TPU v7x, 512 devices: a whole 4x8x8 slice. The times are simulated.
512 devices in a mesh: row: 16 (over y, z_lo), col: 32 (over z_hi, x, core).
Axes of the slice: x: 4, y: 8, z: 8 (z_hi: 4, z_lo: 2; z = z_hi * 2 + z_lo), core: 2. Of those that a mesh axis runs over, the one named last changes fastest.
Arguments:
- tiles: bfloat16 [16, 32, 32, 256, 256], P('row', 'col'), may hold values from -6 to 6
- tile_ids: int32 [16, 32, 2, 32], P('row', 'col'), may hold values from 0 to 7, as said below
- tile_count: int32 [16, 32], P('row', 'col'), may hold values from 8 to 32
- query_degree: int32 [32768], P('row'), may hold values from 1 to 32
- product_degree: int32 [65536], P('col'), may hold values from 1 to 32
- panel: float32 [64, 65536], P(None, ('col', 'row')), may hold values from -6 to 6
Outputs:
- basis: float32 [64, 65536], P(None, ('col', 'row'))
Inputs may be any that keep to these rules, and one draw needn't show every extreme that they name: `tile_ids`: on each device the 32 (tile row, tile column) pairs are distinct; tile row is below 8 and tile column below 8.
All inputs are finite; a program needn't handle non-finite values.
Results may differ from a plain program's by a relative error of at most 0.0042.
Values may be sent and summed in bfloat16 or wider, within the bound.
A program may use at most 64 MiB of HBM per device.

v0:
```python
import math
import jax
import jax.numpy as jnp
from jax import lax
from jax.sharding import PartitionSpec as P

ITERS = 2
HIGH = lax.Precision.HIGHEST


def orthonormal(lifted, gram):
    lower = jnp.linalg.cholesky(gram)
    return lax.linalg.triangular_solve(lower, lifted, left_side=True, lower=True)


def shards(tiles, tile_ids, tile_count, query_degree, product_degree, panel):
    tile_set = tiles[0, 0]
    slot_ids = tile_ids[0, 0]
    live_count = tile_count[0, 0]
    slots = tile_set.shape[0]
    side = tile_set.shape[1]
    width = panel.shape[0]
    query_tiles = query_degree.shape[0] // side
    product_tiles = product_degree.shape[0] // side
    live_slot = (jnp.arange(slots, dtype=jnp.int32) < live_count).astype(jnp.float32)
    row_hot = (slot_ids[0][:, None] == jnp.arange(query_tiles, dtype=jnp.int32)[None, :]).astype(
        jnp.float32
    ) * live_slot[:, None]
    col_hot = (slot_ids[1][:, None] == jnp.arange(product_tiles, dtype=jnp.int32)[None, :]).astype(
        jnp.float32
    ) * live_slot[:, None]
    qscale = 1.0 / jnp.sqrt(query_degree.astype(jnp.float32))
    pscale = 1.0 / jnp.sqrt(product_degree.astype(jnp.float32))
    row_at = lax.axis_index("row")
    col_at = lax.axis_index("col")
    share = panel.shape[1]
    my_pscale = lax.dynamic_slice_in_dim(pscale, row_at * share, share)
    root_count = math.sqrt(product_degree.shape[0] * lax.axis_size("col"))
    current = panel
    for iteration in range(ITERS):
        scaled = (current * my_pscale[None, :]).astype(jnp.bfloat16)
        scaled_block = lax.all_gather(scaled, "row", axis=1, tiled=True)
        picked = jnp.take(scaled_block.reshape(width, product_tiles, side), slot_ids[1], axis=1)
        products = jnp.einsum("rkj,kij->kri", picked, tile_set, preferred_element_type=jnp.float32)
        partial_sum = jnp.einsum("kq,kri->rqi", row_hot, products, precision=HIGH).reshape(
            width, query_tiles * side
        )
        query_share = lax.psum_scatter(partial_sum, "col", scatter_dimension=1, tiled=True)
        columns = query_share.shape[1]
        my_qscale = lax.dynamic_slice_in_dim(qscale, col_at * columns, columns)
        rounded = (query_share * my_qscale[None, :]).astype(jnp.bfloat16)
        query_block = lax.all_gather(rounded, "col", axis=1, tiled=True)
        backward_picked = jnp.take(
            query_block.reshape(width, query_tiles, side), slot_ids[0], axis=1
        )
        backward_products = jnp.einsum(
            "rki,kij->krj", backward_picked, tile_set, preferred_element_type=jnp.float32
        )
        lifted = (
            lax.psum_scatter(
                jnp.einsum("kp,krj->rpj", col_hot, backward_products, precision=HIGH).reshape(
                    width, product_tiles * side
                ),
                "row",
                scatter_dimension=1,
                tiled=True,
            )
            * my_pscale[None, :]
        )
        gram = lax.psum(jnp.einsum("ri,si->rs", lifted, lifted, precision=HIGH), ("row", "col"))
        current = orthonormal(lifted, gram)
    return current * root_count


def solution(mesh):
    in_specs = (
        P("row", "col", None, None, None),
        P("row", "col", None, None),
        P("row", "col"),
        P("row"),
        P("col"),
        P(None, ("col", "row")),
    )
    out_specs = P(None, ("col", "row"))
    return jax.shard_map(shards, mesh=mesh, in_specs=in_specs, out_specs=out_specs, check_vma=False)
```

profile of v0, /device:TPU:24, one launch (start us, length us, event | category | flops | bytes accessed | tf_op | source)
XLA Modules:
  0.0 757.7 jit_solution(1532699937566994767)
XLA Ops:
  10.3 32.3 %all_gather.12 = bf16[64,2048]{1,0:T(8,128)(2,1)S(1)} all-gather(bf16[64,128]{1,0:T(8,128)(2,1)S(1)} %multiply_convert_fusion.2), channel_id=1, replica_groups=mesh['row'=16,'col'=32] {'row'}, dimensions={1}, use_global_device_ids=true | all-gather | bytes 278528 | tf_op jit(solution)/shard_map/all_gather | solution.py:42
  43.2 3.6 fusion.6
  46.8 2.4 fusion.16
  49.1 1.4 copy.55
  51.3 101.7 %reduce-scatter.13.cloned.1.call-done = f32[64,64]{1,0:T(8,128)} async-done(((f32[2048,64]{1,0:T(8,128)}), f32[64,64]{1,0:T(8,128)}) %reduce-scatter.13.cloned.1.call-update) | async-done | bytes 16400
  153.1 0.8 copy.52
  154.0 43.8 %all_gather.13 = bf16[64,2048]{0,1:T(8,128)(2,1)S(1)} all-gather(bf16[64,64]{0,1:T(8,128)(2,1)S(1)} %copy.31), channel_id=1, replica_groups=mesh['row'=16,'col'=32] {'col'}, dimensions={1}, use_global_device_ids=true | all-gather | bytes 270336 | tf_op jit(solution)/shard_map/all_gather | solution.py:52
  198.6 3.1 fusion.4
  201.7 2.4 fusion.12
  204.1 1.0 copy.59
  205.1 67.3 %reduce-scatter.9.cloned.1.call-done = f32[64,128]{1,0:T(8,128)} async-done(((f32[64,2048]{1,0:T(8,128)}), f32[64,128]{1,0:T(8,128)}) %reduce-scatter.9.cloned.1.call-update) | async-done | bytes 32784 | tf_op jit(solution)/shard_map/reduce_scatter | solution.py:60
  272.4 1.0 fusion.51
  273.4 98.9 %psum.14 = f32[64,64]{0,1:T(8,128)S(1)} all-reduce(f32[64,64]{0,1:T(8,128)S(1)} %fusion.51), channel_id=1, replica_groups=mesh['row'=16,'col'=32] {'row','col'}, use_global_device_ids=true, to_apply=%region_2.4 | all-reduce | flops 4096 | bytes 32768 | tf_op jit(solution)/shard_map/psum | solution.py:70
  372.5 5.8 cholesky.44
  379.6 4.9 custom-call.6
  384.5 1.0 fusion.22
  385.6 29.2 %all_gather.14 = bf16[64,2048]{1,0:T(8,128)(2,1)S(1)} all-gather(bf16[64,128]{1,0:T(8,128)(2,1)S(1)} %fusion.22), channel_id=1, replica_groups=mesh['row'=16,'col'=32] {'row'}, dimensions={1}, use_global_device_ids=true | all-gather | bytes 278528 | tf_op jit(solution)/shard_map/all_gather | solution.py:42
  415.4 3.6 fusion.2
  419.0 2.4 fusion.19
  421.4 1.4 copy.56
  422.8 95.3 %reduce-scatter.15.cloned.1.call-done = f32[64,64]{1,0:T(8,128)} async-done(((f32[2048,64]{1,0:T(8,128)}), f32[64,64]{1,0:T(8,128)}) %reduce-scatter.15.cloned.1.call-update) | async-done | bytes 16400
  518.1 0.8 copy.54
  519.0 43.8 %all_gather.15 = bf16[64,2048]{0,1:T(8,128)(2,1)S(1)} all-gather(bf16[64,64]{0,1:T(8,128)(2,1)S(1)} %copy.39), channel_id=1, replica_groups=mesh['row'=16,'col'=32] {'col'}, dimensions={1}, use_global_device_ids=true | all-gather | bytes 270336 | tf_op jit(solution)/shard_map/all_gather | solution.py:52
  563.6 3.1 fusion
  566.7 2.4 fusion.8
  569.1 1.0 copy.60
  570.1 67.3 %reduce-scatter.11.cloned.1.call-done = f32[64,128]{1,0:T(8,128)} async-done(((f32[64,2048]{1,0:T(8,128)}), f32[64,128]{1,0:T(8,128)}) %reduce-scatter.11.cloned.1.call-update) | async-done | bytes 32784 | tf_op jit(solution)/shard_map/reduce_scatter | solution.py:60
  637.4 1.0 fusion.48
  638.4 99.0 %psum.15 = f32[64,64]{0,1:T(8,128)S(1)} all-reduce(f32[64,64]{0,1:T(8,128)S(1)} %fusion.48), channel_id=1, replica_groups=mesh['row'=16,'col'=32] {'row','col'}, use_global_device_ids=true, to_apply=%region_7.11 | all-reduce | flops 4096 | bytes 32768 | tf_op jit(solution)/shard_map/psum | solution.py:70
  737.5 5.8 cholesky.55
  744.7 4.9 custom-call.7
  749.6 1.6 convolution_multiply_fusion
  (38 shorter events, 9.9 us)
Async XLA Ops:
  6.5 146.5 %reduce-scatter.13.cloned.1.call-start = ((), (), s32[]{:S(2)}) async-start(), calls=%async_computation.6 | async-start | bytes 1081344
  50.5 221.9 %reduce-scatter.9.cloned.1.call-start = ((), (), s32[]{:S(2)}) async-start(), calls=%async_computation.4 | async-start | bytes 557056 | tf_op jit(solution)/shard_map/reduce_scatter | solution.py:60
  205.0 313.1 %reduce-scatter.15.cloned.1.call-start = ((), (), s32[]{:S(2)}) async-start(), calls=%async_computation.7 | async-start | bytes 1081344
  422.8 214.6 %reduce-scatter.11.cloned.1.call-start = ((), (), s32[]{:S(2)}) async-start(), calls=%async_computation.5 | async-start | bytes 557056 | tf_op jit(solution)/shard_map/reduce_scatter | solution.py:60
Sparse Core Ops, SparseCore 0:
  50.6 102.3 reduce-scatter.12
  205.2 67.2 reduce-scatter.8
  422.9 95.1 reduce-scatter.14
  570.2 67.1 reduce-scatter.10
where the time goes:
time: 759 us; the launch traced here: 758 us
  blocking collectives  347 us (46%)
  waiting for transfers between devices  332 us (44%)
  matrix products  27.4 us (4%)
  other arithmetic  27.3 us (4%)
  between operations  14 us (2%)
  local copies, waits for them, and re-layouts  10.3 us (1%)
    psum x2, blocking collectives, shards(): lax.psum(jnp.einsum('ri,si->rs', lifted, lifted, precision=HIGH), ('row',...  198 us
    unnamed x6, waiting for transfers between devices  197 us
    reduce_scatter x2, waiting for transfers between devices, shards(): lax.psum_scatter(jnp.einsum('kp,krj->rpj', col_hot, backward_products, pr...  135 us
    all_gather x2, blocking collectives, shards(): query_block = lax.all_gather(rounded, 'col', axis=1, tiled=True)  87.6 us
    all_gather x2, blocking collectives, shards(): scaled_block = lax.all_gather(scaled, 'row', axis=1, tiled=True)  61.5 us
  transfers between devices with their start and end apart: 4, of which 4 were waited for; matrix products, arithmetic and copies ran while one was open for 0% of the time, Pallas kernels for 0%

commit v1 on v0

--- a/solution.py
+++ b/solution.py
@@ -67,7 +67,9 @@
             )
             * my_pscale[None, :]
         )
-        gram = lax.psum(jnp.einsum("ri,si->rs", lifted, lifted, precision=HIGH), ("row", "col"))
+        gram = lax.psum(
+            lax.psum(jnp.einsum("ri,si->rs", lifted, lifted, precision=HIGH), "row"), "col"
+        )
         current = orthonormal(lifted, gram)
     return current * root_count
 

time: 759 us -> 966 us (1.27)
  the two profiles are of different devices: /device:TPU:24 before, /device:TPU:32 now
where the time goes in v1:
time: 966 us; the launch traced here: 965 us
  blocking collectives  555 us (57%)
  waiting for transfers between devices  332 us (34%)
  matrix products  27.4 us (3%)
  other arithmetic  27.2 us (3%)
  between operations  14 us (1%)
  local copies, waits for them, and re-layouts  10.3 us (1%)
    psum x2, blocking collectives, shards(): lax.psum(lax.psum(jnp.einsum('ri,si->rs', lifted, lifted, precision=HIGH)...  278 us
    unnamed x6, waiting for transfers between devices  197 us
    reduce_scatter x2, waiting for transfers between devices, shards(): lax.psum_scatter(jnp.einsum('kp,krj->rpj', col_hot, backward_products, pr...  135 us
    psum x2, blocking collectives, shards(): lax.psum(jnp.einsum('ri,si->rs', lifted, lifted, precision=HIGH), 'row')  124 us
    all_gather x2, blocking collectives, shards(): query_block = lax.all_gather(rounded, 'col', axis=1, tiled=True)  87.6 us
    all_gather x2, blocking collectives, shards(): scaled_block = lax.all_gather(scaled, 'row', axis=1, tiled=True)  64.6 us
  transfers between devices with their start and end apart: 4, of which 4 were waited for; matrix products, arithmetic and copies ran while one was open for 0% of the time, Pallas kernels for 0%

profile of v1, /device:TPU:32, one launch (start us, length us, event | category | flops | bytes accessed | tf_op | source)
XLA Modules:
  0.0 965.4 jit_solution(9216616157615196403)
XLA Ops:
  10.3 33.4 %all_gather.12 = bf16[64,2048]{1,0:T(8,128)(2,1)S(1)} all-gather(bf16[64,128]{1,0:T(8,128)(2,1)S(1)} %multiply_convert_fusion.2), channel_id=1, replica_groups=mesh['row'=16,'col'=32] {'row'}, dimensions={1}, use_global_device_ids=true | all-gather | bytes 278528 | tf_op jit(solution)/shard_map/all_gather | solution.py:42
  44.3 3.6 fusion.6
  47.9 2.4 fusion.16
  50.2 1.4 copy.55
  52.4 100.5 %reduce-scatter.13.cloned.1.call-done = f32[64,64]{1,0:T(8,128)} async-done(((f32[2048,64]{1,0:T(8,128)}), f32[64,64]{1,0:T(8,128)}) %reduce-scatter.13.cloned.1.call-update) | async-done | bytes 16400
  153.9 43.8 %all_gather.13 = bf16[64,2048]{0,1:T(8,128)(2,1)S(1)} all-gather(bf16[64,64]{0,1:T(8,128)(2,1)S(1)} %copy.31), channel_id=1, replica_groups=mesh['row'=16,'col'=32] {'col'}, dimensions={1}, use_global_device_ids=true | all-gather | bytes 270336 | tf_op jit(solution)/shard_map/all_gather | solution.py:52
  198.5 3.1 fusion.4
  201.6 2.4 fusion.12
  203.9 1.0 copy.59
  205.0 67.3 %reduce-scatter.9.cloned.1.call-done = f32[64,128]{1,0:T(8,128)} async-done(((f32[64,2048]{1,0:T(8,128)}), f32[64,128]{1,0:T(8,128)}) %reduce-scatter.9.cloned.1.call-update) | async-done | bytes 32784 | tf_op jit(solution)/shard_map/reduce_scatter | solution.py:60
  272.3 1.0 fusion.51
  273.3 62.2 %psum.28 = f32[64,64]{0,1:T(8,128)S(1)} all-reduce(f32[64,64]{0,1:T(8,128)S(1)} %fusion.51), channel_id=1, replica_groups=mesh['row'=16,'col'=32] {'row'}, use_global_device_ids=true, to_apply=%region_2.4 | all-reduce | flops 4096 | bytes 32768 | tf_op jit(solution)/shard_map/psum | solution.py:71
  335.5 139.0 %psum.29 = f32[64,64]{0,1:T(8,128)S(1)} all-reduce(f32[64,64]{0,1:T(8,128)S(1)} %psum.28), channel_id=1, replica_groups=mesh['row'=16,'col'=32] {'col'}, use_global_device_ids=true, to_apply=%region_3.5 | all-reduce | flops 4096 | bytes 32768 | tf_op jit(solution)/shard_map/psum | solution.py:70
  474.6 5.8 cholesky.44
  481.8 4.9 custom-call.6
  486.7 1.0 fusion.22
  487.7 31.2 %all_gather.14 = bf16[64,2048]{1,0:T(8,128)(2,1)S(1)} all-gather(bf16[64,128]{1,0:T(8,128)(2,1)S(1)} %fusion.22), channel_id=1, replica_groups=mesh['row'=16,'col'=32] {'row'}, dimensions={1}, use_global_device_ids=true | all-gather | bytes 278528 | tf_op jit(solution)/shard_map/all_gather | solution.py:42
  519.5 3.6 fusion.2
  523.1 2.4 fusion.19
  525.5 1.4 copy.56
  526.9 96.6 %reduce-scatter.15.cloned.1.call-done = f32[64,64]{1,0:T(8,128)} async-done(((f32[2048,64]{1,0:T(8,128)}), f32[64,64]{1,0:T(8,128)}) %reduce-scatter.15.cloned.1.call-update) | async-done | bytes 16400
  624.4 43.8 %all_gather.15 = bf16[64,2048]{0,1:T(8,128)(2,1)S(1)} all-gather(bf16[64,64]{0,1:T(8,128)(2,1)S(1)} %copy.39), channel_id=1, replica_groups=mesh['row'=16,'col'=32] {'col'}, dimensions={1}, use_global_device_ids=true | all-gather | bytes 270336 | tf_op jit(solution)/shard_map/all_gather | solution.py:52
  669.1 3.1 fusion
  672.2 2.4 fusion.8
  674.5 1.0 copy.60
  675.5 67.4 %reduce-scatter.11.cloned.1.call-done = f32[64,128]{1,0:T(8,128)} async-done(((f32[64,2048]{1,0:T(8,128)}), f32[64,128]{1,0:T(8,128)}) %reduce-scatter.11.cloned.1.call-update) | async-done | bytes 32784 | tf_op jit(solution)/shard_map/reduce_scatter | solution.py:60
  742.9 1.0 fusion.48
  743.9 62.1 %psum.30 = f32[64,64]{0,1:T(8,128)S(1)} all-reduce(f32[64,64]{0,1:T(8,128)S(1)} %fusion.48), channel_id=1, replica_groups=mesh['row'=16,'col'=32] {'row'}, use_global_device_ids=true, to_apply=%region_8.0 | all-reduce | flops 4096 | bytes 32768 | tf_op jit(solution)/shard_map/psum | solution.py:71
  806.0 139.0 %psum.31 = f32[64,64]{0,1:T(8,128)S(1)} all-reduce(f32[64,64]{0,1:T(8,128)S(1)} %psum.30), channel_id=1, replica_groups=mesh['row'=16,'col'=32] {'col'}, use_global_device_ids=true, to_apply=%region_9.13 | all-reduce | flops 4096 | bytes 32768 | tf_op jit(solution)/shard_map/psum | solution.py:70
  945.2 5.8 cholesky.55
  952.3 4.9 custom-call.7
  957.2 1.6 convolution_multiply_fusion
  (40 shorter events, 11.6 us)
Async XLA Ops:
  6.5 146.4 %reduce-scatter.13.cloned.1.call-start = ((), (), s32[]{:S(2)}) async-start(), calls=%async_computation.6 | async-start | bytes 1081344
  51.6 220.7 %reduce-scatter.9.cloned.1.call-start = ((), (), s32[]{:S(2)}) async-start(), calls=%async_computation.4 | async-start | bytes 557056 | tf_op jit(solution)/shard_map/reduce_scatter | solution.py:60
  204.9 418.6 %reduce-scatter.15.cloned.1.call-start = ((), (), s32[]{:S(2)}) async-start(), calls=%async_computation.7 | async-start | bytes 1081344
  526.8 216.0 %reduce-scatter.11.cloned.1.call-start = ((), (), s32[]{:S(2)}) async-start(), calls=%async_computation.5 | async-start | bytes 557056 | tf_op jit(solution)/shard_map/reduce_scatter | solution.py:60
Sparse Core Ops, SparseCore 0:
  51.7 101.1 reduce-scatter.12
  205.0 67.1 reduce-scatter.8
  527.0 96.4 reduce-scatter.14
  675.6 67.2 reduce-scatter.10
